TPU v7x, 512 devices: a whole 4x4x16 slice. The times are simulated.
512 devices in a mesh: grp: 16 (over z), sub: 32 (over x, y, core).
Axes of the slice: x: 4, y: 4, z: 16, core: 2. Of those that a mesh axis runs over, the one named last changes fastest.
Arguments:
- leaf_bases: bfloat16 [6144, 256, 128], P(('grp', 'sub')), may hold values from -6 to 6
- leaf_transfers: bfloat16 [6144, 128, 128], P(('grp', 'sub')), may hold values from -1 to 2
- leaf_blocks: bfloat16 [6144, 6, 128, 128], P(('grp', 'sub')), may hold values from -6 to 6
- leaf_partner_dev: int32 [6144, 6], P(('grp', 'sub')), may hold values from 0 to 31, all different within a row; in each aligned block of 12 rows (0 to 11, 12 to 23, ...) at most 5 rows name the same one
- leaf_partner_slot: int32 [6144, 6], P(('grp', 'sub')), may hold values from 0 to 11
- parent_blocks: bfloat16 [3072, 3, 128, 128], P(('grp', 'sub')), may hold values from -6 to 6
- parent_partner_group: int32 [3072, 3], P(('grp', 'sub')), may hold values from 0 to 15, all different within a row; in each aligned block of 6 rows (0 to 5, 6 to 11, ...) at most 3 rows name the same one
- parent_partner_slot: int32 [3072, 3], P(('grp', 'sub')), may hold values from 0 to 5
- leaf_start: float32 [64, 128], replicated, may hold values from -6 to 6
- parent_start: float32 [64, 128], replicated, may hold values from -6 to 6
Outputs:
- new_leaf_bases: bfloat16 [6144, 64, 256], P(('grp', 'sub'))
- new_leaf_blocks: bfloat16 [6144, 6, 4096], P(('grp', 'sub'))
- new_parent_blocks: bfloat16 [3072, 3, 4096], P(('grp', 'sub'))
Inputs may be any that keep to these rules, and one draw needn't show every extreme that they name: `leaf_partner_dev`: one leaf's partners lie on different devices of its group; among the leaves of one device no index appears more than 5 times, and that count is reached on some device. `parent_partner_group`: one parent's partners lie in different groups; among the parents of one device no group appears more than 3 times, and that count is reached on some device.
All inputs are finite; a program needn't handle non-finite values.
Results may differ from a plain program's by a relative error of at most 0.033.
Values may be sent and summed in bfloat16 or wider, within the bound.
A program may use at most 64 MiB of HBM per device.

v0:
```python
import jax
import jax.numpy as jnp
from jax import lax
from jax.sharding import PartitionSpec as P

TOP_PRECISION = lax.Precision.HIGHEST


def partner(block, axis, apart):
    count = lax.axis_size(axis)
    route = []
    for low in range(count):
        high = low | 1 << apart
        if high != low and high < count:
            route += [(low, high), (high, low)]
    return lax.ppermute(block, axis, route)


def subspace(weight, start_rows):
    basis_rows = jnp.broadcast_to(start_rows, (weight.shape[0],) + start_rows.shape)
    image_rows = jnp.einsum("brn,bnm->brm", basis_rows, weight, precision=TOP_PRECISION)
    image_rows = jnp.einsum("brn,bnm->brm", image_rows, weight, precision=TOP_PRECISION)
    cross_gram = jnp.einsum("brn,bsn->brs", image_rows, image_rows, precision=TOP_PRECISION)
    factor = jnp.linalg.cholesky(cross_gram)
    return jax.scipy.linalg.solve_triangular(factor, image_rows, lower=True)


def shards(
    leaf_bases,
    leaf_transfers,
    leaf_blocks,
    leaf_partner_dev,
    leaf_partner_slot,
    parent_blocks,
    parent_partner_group,
    parent_partner_slot,
    leaf_start,
    parent_start,
):
    leaf_count = leaf_blocks.shape[0]
    leaf_links = leaf_blocks.shape[1]
    half_count = parent_blocks.shape[0]
    parent_links = parent_blocks.shape[1]
    rank_new = leaf_start.shape[0]
    rank_old = leaf_start.shape[1]
    member = lax.axis_index("sub") % 2
    parent_weight = jnp.einsum(
        "pckl,pcml->pkm", parent_blocks, parent_blocks, preferred_element_type=jnp.float32
    )
    partner_weight = partner(parent_weight.astype(jnp.bfloat16), "sub", 0).astype(
        parent_weight.dtype
    )
    descended = jnp.where(
        member == 0,
        jnp.concatenate([parent_weight, partner_weight], axis=0),
        jnp.concatenate([partner_weight, parent_weight], axis=0),
    )
    weight = jnp.einsum(
        "jckl,jcml->jkm", leaf_blocks, leaf_blocks, preferred_element_type=jnp.float32
    )
    transfers = leaf_transfers.astype(jnp.float32)
    carried = jnp.einsum("jka,jab->jkb", transfers, descended, precision=TOP_PRECISION)
    weight = weight + jnp.einsum("jkb,jmb->jkm", carried, transfers, precision=TOP_PRECISION)
    change = subspace(weight, leaf_start).astype(jnp.bfloat16)
    projected = jnp.einsum(
        "jrk,jkm->jrm", change, leaf_transfers, preferred_element_type=jnp.float32
    )
    sent_rows = lax.dynamic_slice_in_dim(projected, (1 - member) * half_count, half_count, 0)
    received_rows = partner(sent_rows.astype(jnp.bfloat16), "sub", 0).astype(sent_rows.dtype)
    kept_rows = lax.dynamic_slice_in_dim(projected, member * half_count, half_count, 0)
    stacked = jnp.where(
        member == 0,
        jnp.concatenate([kept_rows, received_rows], axis=1),
        jnp.concatenate([received_rows, kept_rows], axis=1),
    )
    new_leaf_bases = jnp.einsum(
        "jrk,jnk->jrn", change, leaf_bases, preferred_element_type=jnp.float32
    ).astype(jnp.bfloat16)
    leaf_midpoint = jnp.einsum(
        "jrk,jckl->jcrl", change, leaf_blocks, preferred_element_type=jnp.float32
    ).astype(jnp.bfloat16)
    parent_left = jnp.einsum("prk,pkm->prm", stacked, parent_weight, precision=TOP_PRECISION)
    parent_gram = jnp.einsum("prm,psm->prs", parent_left, stacked, precision=TOP_PRECISION)
    parent_rows = subspace(parent_gram, parent_start)
    parent_change = jnp.einsum(
        "prs,psk->prk", parent_rows, stacked, precision=TOP_PRECISION
    ).astype(jnp.bfloat16)
    parent_midpoint = jnp.einsum(
        "prk,pckl->pcrl", parent_change, parent_blocks, preferred_element_type=jnp.float32
    ).astype(jnp.bfloat16)
    everyone = lax.all_gather(change, "sub", axis=0, tiled=True)
    distant_site = everyone[(leaf_partner_dev * leaf_count + leaf_partner_slot).reshape(-1)]
    distant_site = distant_site.reshape(leaf_count, leaf_links, rank_new, rank_old)
    new_leaf_blocks = jnp.einsum(
        "jcrl,jcsl->jcrs", leaf_midpoint, distant_site, preferred_element_type=jnp.float32
    ).astype(jnp.bfloat16)
    new_leaf_blocks = new_leaf_blocks.reshape(leaf_count, leaf_links, rank_new * rank_new)
    everyone_parents = lax.all_gather(parent_change, "grp", axis=0, tiled=True)
    distant_parents = everyone_parents[
        (parent_partner_group * half_count + parent_partner_slot).reshape(-1)
    ]
    distant_parents = distant_parents.reshape(half_count, parent_links, rank_new, rank_old)
    new_parent_blocks = jnp.einsum(
        "juog,juqg->juoq", parent_midpoint, distant_parents, preferred_element_type=jnp.float32
    ).astype(jnp.bfloat16)
    new_parent_blocks = new_parent_blocks.reshape(half_count, parent_links, rank_new * rank_new)
    return (new_leaf_bases, new_leaf_blocks, new_parent_blocks)


def solution(mesh):
    placed = (
        P(("grp", "sub"), None, None),
        P(("grp", "sub"), None, None),
        P(("grp", "sub"), None, None, None),
        P(("grp", "sub"), None),
        P(("grp", "sub"), None),
        P(("grp", "sub"), None, None, None),
        P(("grp", "sub"), None),
        P(("grp", "sub"), None),
        P(),
        P(),
    )
    return jax.shard_map(
        shards,
        mesh=mesh,
        in_specs=placed,
        out_specs=(
            P(("grp", "sub"), None, None),
            P(("grp", "sub"), None, None),
            P(("grp", "sub"), None, None),
        ),
        check_vma=False,
    )
```

profile of v0, /device:TPU:1, one launch (start us, length us, event | category | flops | bytes accessed | tf_op | source)
XLA Modules:
  0.0 399.2 jit_solution(17246581851803399312)
XLA Ops:
  7.2 0.0 copy-start
  7.2 0.0 all-gather.5.cloned.1.call-start
  7.2 1.8 fusion.30
  9.0 8.8 %collective-permute-start = (bf16[6,128,128]{2,1,0:T(8,128)(2,1)S(1)}, bf16[6,128,128]{2,1,0:T(8,128)(2,1)S(1)}, u32[]{:S(2)}, u32[]{:S(2)}) collective-permute-start(bf16[6,128,128]{2,1,0:T(8,128)(2,1)S(1)} %get-tuple-element.3), channel_id=1, source_target_pairs={{0,1},{1,0},{2,3},{3,2},{4,5},{5,4},{6,7},{7,6},{8,9},{9,8},{10,11... | collective-permute-start | bytes 589832 | tf_op jit(solution)/shard_map/ppermute | solution.py:16
  17.8 0.0 copy-done
  17.8 0.0 copy-start.4
  17.8 1.7 convolution_bitcast_fusion
  19.5 0.0 collective-permute-done
  19.6 0.0 copy-done.4
  19.6 0.0 copy-start.9
  19.6 0.6 fusion.2
  20.2 0.4 copy-done.5
  20.6 0.9 convolution_add_fusion
  21.6 0.0 copy-done.9
  21.6 0.8 fusion.16
  22.4 0.8 fusion.31
  23.2 1.5 fusion.32
  24.7 1.9 copy.33
  26.6 1.9 fusion.9
  28.5 71.8 %custom-call.16 = f32[12,64,64]{2,1,0:T(8,128)} custom-call(f32[12,64,64]{2,1,0:T(8,128)} %fusion.9), custom_call_target="Cholesky" | custom-call | tf_op jit(solution)/shard_map/jit(cholesky)/cholesky | solution.py:24
  100.3 1.1 select_reduce_fusion
  101.3 0.1 compare_reduce_fusion
  101.4 1.9 select_bitcast_fusion
  103.3 60.4 %custom-call.17 = f32[12,1,64,64]{2,3,1,0:T(8,128)} custom-call(f32[12,1,64,64]{3,2,1,0:T(8,128)} %select_bitcast_fusion), custom_call_target="InvertDiagBlocksLowerTriangular" | custom-call | tf_op jit(solution)/shard_map/jit(_solve_triangular)/vmap()/triangular_solve | solution.py:25
  163.7 1.8 convolution_convert_fusion.5
  165.5 0.0 copy-start.2
  165.5 0.0 copy-start.10
  165.5 1.3 fusion.33
  166.8 2.1 collective-permute-start.1
  169.0 0.0 copy-start.6
  169.0 1.0 collective-permute-done.1
  170.0 0.0 copy-start.7
  170.0 0.5 fusion.23
  170.6 0.9 fusion.22
  171.5 0.0 copy-done.10
  171.5 0.5 fusion.20
  172.0 0.5 fusion.34
  172.5 0.4 fusion.35
  173.0 0.8 copy.36
  173.8 1.7 fusion.15
  175.5 35.9 %custom-call.18 = f32[6,64,64]{2,1,0:T(8,128)S(1)} custom-call(f32[6,64,64]{2,1,0:T(8,128)} %fusion.15), custom_call_target="Cholesky" | custom-call | tf_op jit(solution)/shard_map/jit(cholesky)/cholesky | solution.py:24
  211.4 0.1 compare_reduce_fusion.1
  211.5 0.8 select_bitcast_fusion.1
  212.3 30.2 %custom-call.19 = f32[6,1,64,64]{2,3,1,0:T(8,128)S(1)} custom-call(f32[6,1,64,64]{3,2,1,0:T(8,128)} %select_bitcast_fusion.1), custom_call_target="InvertDiagBlocksLowerTriangular" | custom-call | tf_op jit(solution)/shard_map/jit(_solve_triangular)/vmap()/triangular_solve | solution.py:25
  242.5 0.5 fusion.13
  243.0 2.3 convolution_convert_fusion.6
  245.4 0.0 all-gather.5.cloned.1.call-update
  245.4 0.0 all-gather.3.cloned.1.call-start
  245.5 0.7 all-gather.3.cloned.1.call-update
  246.2 0.7 multiply_add_fusion.1
  246.9 0.1 copy.38
  247.0 0.1 reshape.105
  247.0 0.7 multiply_add_fusion
  247.7 0.1 copy.35
  247.8 0.1 reshape.102
  248.0 2.3 convolution_convert_fusion.2
  250.3 56.5 %all-gather.5.cloned.1.call-done = bf16[96,64,128]{2,1,0:T(8,128)(2,1)} async-done(((bf16[6,64,128]{2,1,0:T(8,128)(2,1)}), bf16[96,64,128]{2,1,0:T(8,128)(2,1)}) %all-gather.5.cloned.1.call-update) | async-done | bytes 1572880 | tf_op jit(solution)/shard_map/all_gather | solution.py:98
  306.8 2.0 gather_fusion.1
  308.8 1.1 convolution_convert_fusion.3
  310.0 1.9 reshape.107
  311.8 69.6 %all-gather.3.cloned.1.call-done = bf16[384,64,128]{2,1,0:T(8,128)(2,1)} async-done(((bf16[12,64,128]{2,1,0:T(8,128)(2,1)}), bf16[384,64,128]{2,1,0:T(8,128)(2,1)}) %all-gather.3.cloned.1.call-update) | async-done | bytes 6291472 | tf_op jit(solution)/shard_map/all_gather | solution.py:91
  381.5 4.6 %gather_fusion = bf16[72,64,128]{2,1,0:T(8,128)(2,1)} fusion(bf16[384,64,128]{2,1,0:T(8,128)(2,1)} %all-gather.3.cloned.1.call-done, s32[1024]{0:T(1024)S(1)} %pad_clamp_fusion.1), kind=kCustom, calls=%fused_computation | custom fusion | bytes 2359584 | tf_op jit(solution)/shard_map/gather | solution.py:92
  386.1 3.4 convolution_convert_fusion
  389.5 2.9 reshape.104
  (21 shorter events, 0.2 us)
Async XLA Ops:
  7.2 10.7 %copy-start = (bf16[12,6,128,128]{3,2,1,0:T(8,128)(2,1)S(1)}, bf16[12,6,128,128]{3,2,1,0:T(8,128)(2,1)}, u32[]{:S(2)}) copy-start(bf16[12,6,128,128]{3,2,1,0:T(8,128)(2,1)} %param.12) | copy-start | bytes 7077892
  7.2 299.6 %all-gather.5.cloned.1.call-start = ((), (), s32[]{:S(2)}) async-start(), calls=%async_computation.1 | async-start | bytes 1671168 | tf_op jit(solution)/shard_map/all_gather | solution.py:98
  9.0 10.5 %collective-permute-start = (bf16[6,128,128]{2,1,0:T(8,128)(2,1)S(1)}, bf16[6,128,128]{2,1,0:T(8,128)(2,1)S(1)}, u32[]{:S(2)}, u32[]{:S(2)}) collective-permute-start(bf16[6,128,128]{2,1,0:T(8,128)(2,1)S(1)} %get-tuple-element.3), channel_id=1, source_target_pairs={{0,1},{1,0},{2,3},{3,2},{4,5},{5,4},{6,7},{7,6},{8,9},{9,8},{10,11... | collective-permute-start | bytes 589832 | tf_op jit(solution)/shard_map/ppermute | solution.py:16
  17.8 1.7 copy-start.4
  19.5 1.1 copy-start.5
  19.6 2.0 copy-start.9
  165.5 6.5 %copy-start.2 = (bf16[12,64,128]{2,1,0:T(8,128)(2,1)}, bf16[12,64,128]{2,1,0:T(8,128)(2,1)S(1)}, u32[]{:S(2)}) copy-start(bf16[12,64,128]{2,1,0:T(8,128)(2,1)S(1)} %convolution_convert_fusion.5) | copy-start | bytes 589828
  165.5 6.1 %copy-start.10 = (f32[64,128]{1,0:T(8,128)S(1)}, f32[64,128]{1,0:T(8,128)}, u32[]{:S(2)}) copy-start(f32[64,128]{1,0:T(8,128)} %param.19) | copy-start | bytes 98308
  166.8 3.2 collective-permute-start.1
  169.0 3.5 copy-start.6
  170.0 2.5 copy-start.7
  172.5 75.5 %copy-start.3 = (bf16[12,64,128]{2,1,0:T(8,128)(2,1)S(1)}, bf16[12,64,128]{2,1,0:T(8,128)(2,1)}, u32[]{:S(2)}) copy-start(bf16[12,64,128]{2,1,0:T(8,128)(2,1)} %copy-done.2) | copy-start | bytes 589828
  173.8 135.0 %copy-start.1 = (bf16[6,3,128,128]{3,2,1,0:T(8,128)(2,1)S(1)}, bf16[6,3,128,128]{3,2,1,0:T(8,128)(2,1)}, u32[]{:S(2)}) copy-start(bf16[6,3,128,128]{3,2,1,0:T(8,128)(2,1)} %param.15) | copy-start | bytes 1769476
  245.4 63.4 %copy-start.8 = (bf16[6,64,128]{2,1,0:T(8,128)(2,1)S(1)}, bf16[6,64,128]{2,1,0:T(8,128)(2,1)}, u32[]{:S(2)}) copy-start(bf16[6,64,128]{2,1,0:T(8,128)(2,1)} %convolution_convert_fusion.6) | copy-start | bytes 294916
  245.4 136.1 %all-gather.3.cloned.1.call-start = ((), (), s32[]{:S(2)}) async-start(), calls=%async_computation | async-start | bytes 6488064 | tf_op jit(solution)/shard_map/all_gather | solution.py:91
Sparse Core Ops, SparseCore 0:
  245.5 61.2 all-gather.4
  309.9 71.5 all-gather.2
where the time goes:
time: 400 us; the launch traced here: 399 us
  other arithmetic  207 us (52%)
  waiting for transfers between devices  128 us (32%)
  matrix products  23.6 us (6%)
  local copies, waits for them, and re-layouts  15 us (4%)
  between operations  14.4 us (4%)
  starting transfers between devices  11 us (3%)
    another operation x7, other arithmetic, subspace(): factor = jnp.linalg.cholesky(cross_gram)  109 us
    another operation x5, other arithmetic, subspace(): return jax.scipy.linalg.solve_triangular(factor, image_rows, lower=True)  93.2 us
    all_gather x1, waiting for transfers between devices, shards(): everyone = lax.all_gather(change, 'sub', axis=0, tiled=True)  69.6 us
    all_gather x1, waiting for transfers between devices, shards(): everyone_parents = lax.all_gather(parent_change, 'grp', axis=0, tiled=True)  56.5 us
    ppermute x2, starting transfers between devices, partner(): return lax.ppermute(block, axis, route)  10.9 us
  transfers between devices with their start and end apart: 4, of which 3 were waited for; matrix products, arithmetic and copies ran while one was open for 3% of the time, Pallas kernels for 0%

commit v1 on v0

v1 whole, which is shorter than its diff:
```python
import functools

import jax
import jax.numpy as jnp
from jax import lax
from jax.experimental import pallas as pl
from jax.experimental.pallas import tpu as pltpu
from jax.sharding import PartitionSpec as P

HIGHEST = lax.Precision.HIGHEST
MESH = pl.DeviceIdType.MESH
F32 = jnp.float32
BF16 = jnp.bfloat16
SIDE = 4


def nt(left, right, precision=None):
    return lax.dot_general(
        left, right, (((1,), (1,)), ((), ())), precision=precision, preferred_element_type=F32
    )


def nn(left, right, precision=None):
    return lax.dot_general(
        left, right, (((1,), (0,)), ((), ())), precision=precision, preferred_element_type=F32
    )


def partner(block, axis, apart):
    count = lax.axis_size(axis)
    route = []
    for low in range(count):
        high = low | 1 << apart
        if high != low and high < count:
            route += [(low, high), (high, low)]
    return lax.ppermute(block, axis, route)


def eliminate(joined):
    count, rows, width = joined.shape
    lane = rows
    tiles = [joined[:, 8 * i : 8 * i + 8, :] for i in range(rows // 8)]
    full = (count, 8, width)
    place = lax.broadcasted_iota(jnp.int32, full, 1)
    for at in range(rows // 8):
        scale = jnp.zeros(full, F32)
        for inner in range(8):
            k = lane + at * 8 + inner
            tile = tiles[at]
            column = jnp.broadcast_to(tile[:, :, k : k + 1], full)
            pivot = jnp.broadcast_to(column[:, inner : inner + 1, :], full)
            row = jnp.broadcast_to(tile[:, inner : inner + 1, :], full) * (1.0 / pivot)
            scale = jnp.where(place == inner, lax.rsqrt(pivot), scale)
            tiles[at] = tile - jnp.where(place > inner, column, 0.0) * row
            for i in range(at + 1, rows // 8):
                tiles[i] = tiles[i] - jnp.broadcast_to(tiles[i][:, :, k : k + 1], full) * row
        tiles[at] = tiles[at] * scale
    return jnp.concatenate(tiles, axis=1)


def begin_subspace(start, weight):
    rows, width = start.shape
    image = nn(nn(start, weight, HIGHEST), weight, HIGHEST)
    first = lax.broadcasted_iota(jnp.int32, (rows, width), 0)
    second = lax.broadcasted_iota(jnp.int32, (rows, width), 1)
    unit = jnp.where(first == second, 1.0, 0.0)
    gram = nt(image, jnp.concatenate([jnp.zeros_like(image), image], axis=0), HIGHEST)
    return image, gram + unit


def end_subspace(joined, image):
    return nn(joined, jnp.concatenate([image, jnp.zeros_like(image)], axis=0), HIGHEST)


def parent_weight_kernel(blocks_ref, weight_ref, sent_ref):
    count, links = blocks_ref.shape[:2]

    @pl.loop(0, count)
    def _(p):
        total = nt(blocks_ref[p, 0], blocks_ref[p, 0])
        for c in range(1, links):
            total = total + nt(blocks_ref[p, c], blocks_ref[p, c])
        weight_ref[p] = total
        sent_ref[p] = total.astype(BF16)


def leaf_weight_kernel(blocks_ref, weight_ref):
    count, links = blocks_ref.shape[:2]

    @pl.loop(0, count)
    def _(t):
        total = None
        for c in range(0, links, 2):
            pair = jnp.concatenate([blocks_ref[t, c], blocks_ref[t, c + 1]], axis=1)
            product = nt(pair, pair)
            total = product if total is None else total + product
        weight_ref[t] = total


def leaf_kernel(
    weight_ref, own_ref, other_ref, transfers_ref, start_ref,
    change_ref, kept_ref, sent_ref, joined_ref, image_ref,
):
    count = weight_ref.shape[0]
    half = own_ref.shape[0]
    member = lax.rem(lax.axis_index("sub"), 2)

    def prepare(t, descended):
        transfer = transfers_ref[t].astype(F32)
        carried = nn(transfer, descended, HIGHEST)
        weight = weight_ref[t] + nt(carried, transfer, HIGHEST)
        image_ref[t], joined_ref[t] = begin_subspace(start_ref[...], weight)

    @pl.loop(0, half)
    def _(p):
        prepare(member * half + p, own_ref[p])
        prepare((1 - member) * half + p, other_ref[p].astype(F32))

    joined_ref[...] = eliminate(joined_ref[...])

    def finish(t):
        change = end_subspace(joined_ref[t], image_ref[t]).astype(BF16)
        change_ref[t] = change
        return nn(change, transfers_ref[t])

    @pl.loop(0, half)
    def _(p):
        kept_ref[p] = finish(member * half + p)
        sent_ref[p] = finish((1 - member) * half + p).astype(BF16)


def parent_kernel(weight_ref, kept_ref, received_ref, start_ref, change_ref, joined_ref, image_ref, stacked_ref):
    count = weight_ref.shape[0]
    first = lax.rem(lax.axis_index("sub"), 2) == 0

    @pl.loop(0, count)
    def _(p):
        kept, received = kept_ref[p], received_ref[p].astype(F32)
        stacked = jnp.concatenate(
            [jnp.where(first, kept, received), jnp.where(first, received, kept)], axis=0
        )
        stacked_ref[p] = stacked
        gram = nt(nn(stacked, weight_ref[p], HIGHEST), stacked, HIGHEST)
        image_ref[p], joined_ref[p] = begin_subspace(start_ref[...], gram)

    joined_ref[...] = eliminate(joined_ref[...])

    @pl.loop(0, count)
    def _(p):
        rows = end_subspace(joined_ref[p], image_ref[p])
        change_ref[p] = nn(rows, stacked_ref[p], HIGHEST).astype(BF16)


def couple_kernel(
    groups,
    leaf_dev_ref, leaf_slot_ref, parent_group_ref, parent_slot_ref,
    change_ref, parent_change_ref, bases_ref, leaf_blocks_ref, parent_blocks_ref,
    bases_out, leaf_out, parent_out,
    leaves, parents, half_rows, parent_half_rows, staged,
    local_sem, leaf_send, leaf_recv, ring_send, ring_recv,
):
    count, links = leaf_blocks_ref.shape[:2]
    parent_count, parent_links = parent_blocks_ref.shape[:2]
    rank = change_ref.shape[1]
    part = count // 2
    chunk = parent_count // 2
    sub, grp = lax.axis_index("sub"), lax.axis_index("grp")
    across, along, core = sub // (2 * SIDE), (sub // 2) % SIDE, sub % 2

    def site(x, y, c):
        return ((x + SIDE) % SIDE * SIDE + (y + SIDE) % SIDE) * 2 + c

    def near(h, outer, inner):
        if h == 0:
            return site(across + inner, along + outer, core)
        return site(across + outer, along + inner, core)

    outer_at = (along, across)
    inner_at = (across, along)

    def row_start(h, outer):
        return ((h * 2 + core) * SIDE + (outer + SIDE) % SIDE) * SIDE * part

    def block_start(h, outer, inner):
        return row_start(h, outer) + (inner + SIDE) % SIDE * part

    up, down = (grp + 1) % groups, (grp + groups - 1) % groups
    sibling = site(across, along, 1 - core)

    barrier = pltpu.get_barrier_semaphore()
    for target in (near(0, 0, 1), near(0, 0, -1), near(0, 1, 0), near(0, -1, 0), sibling):
        pl.semaphore_signal(barrier, inc=1, device_id={"sub": target}, device_id_type=MESH)
    for target in (up, down):
        pl.semaphore_signal(barrier, inc=1, device_id={"grp": target}, device_id_type=MESH)

    started = []

    def send_leaf(number, src, start, size, target):
        copy = pltpu.make_async_remote_copy(
            src_ref=src,
            dst_ref=leaves.at[pl.ds(start, size)],
            send_sem=leaf_send.at[number],
            recv_sem=leaf_recv.at[number],
            device_id={"sub": target},
            device_id_type=MESH,
        )
        copy.start()
        started.append(copy)
        return copy

    def pass_leaf(number, start, size, target):
        return send_leaf(number, leaves.at[pl.ds(start, size)], start, size, target)

    def send_parent(way, step, piece):
        number = (way * 8 + step) * 2 + piece
        origin = (grp - step + groups) % groups if way == 0 else (grp + step) % groups
        at = origin * parent_count + piece * chunk
        src = parent_change_ref.at[pl.ds(piece * chunk, chunk)] if step == 0 else parents.at[pl.ds(at, chunk)]
        copy = pltpu.make_async_remote_copy(
            src_ref=src,
            dst_ref=parents.at[pl.ds(at, chunk)],
            send_sem=ring_send.at[number],
            recv_sem=ring_recv.at[number],
            device_id={"grp": up if way == 0 else down},
            device_id_type=MESH,
        )
        copy.start()
        started.append(copy)
        return copy

    local = [
        pltpu.make_async_copy(
            change_ref.at[pl.ds(h * part, part)],
            leaves.at[pl.ds(block_start(h, outer_at[h], inner_at[h]), part)],
            local_sem.at[h],
        )
        for h in range(2)
    ]
    local.append(
        pltpu.make_async_copy(
            parent_change_ref, parents.at[pl.ds(grp * parent_count, parent_count)], local_sem.at[2]
        )
    )
    for copy in local:
        copy.start()

    pl.semaphore_wait(barrier, 7)

    inner_up, inner_down = [], []
    for h in range(2):
        own = change_ref.at[pl.ds(h * part, part)]
        start = block_start(h, outer_at[h], inner_at[h])
        inner_up.append(send_leaf(h * 2, own, start, part, near(h, 0, 1)))
        inner_down.append(send_leaf(h * 2 + 1, own, start, part, near(h, 0, -1)))
    ring = {}
    for piece in range(2):
        for way in range(2):
            ring[way, 0, piece] = send_parent(way, 0, piece)

    def ring_step(step):
        for piece in range(2):
            for way in range(2):
                if (way, step, piece) not in ring:
                    continue
                ring[way, step, piece].wait_recv()
                if step < groups // 2 - 2 or (step == groups // 2 - 2 and way == piece):
                    ring[way, step + 1, piece] = send_parent(way, step + 1, piece)

    row = lax.broadcasted_iota(jnp.int32, (rank, rank), 0)
    column = lax.broadcasted_iota(jnp.int32, (rank, rank), 1)
    low = rank // 2
    order = jnp.where(row < low, 2 * row, 2 * (row - low) + 1)
    shuffle = jnp.where(column == order, 1.0, 0.0).astype(BF16)

    @pl.loop(0, count)
    def _(t):
        bases_out[t] = nt(change_ref[t], bases_ref[t]).astype(BF16)

    for h in range(2):
        inner_up[h].wait_recv()
        inner_down[h].wait_recv()
    second_up, second_down = [], []
    cut = part // 2
    for h in range(2):
        outer, inner = outer_at[h], inner_at[h]
        second_up.append(
            pass_leaf(4 + h * 2, block_start(h, outer, inner - 1), cut, near(h, 0, 1))
        )
        second_down.append(
            pass_leaf(5 + h * 2, block_start(h, outer, inner + 1) + cut, part - cut, near(h, 0, -1))
        )
    ring_step(0)

    @pl.loop(0, parent_count)
    def _(p):
        mixed = nn(shuffle, parent_change_ref[p]).astype(BF16)
        for c in range(parent_links):
            parent_half_rows[p * parent_links + c] = nn(mixed, parent_blocks_ref[p, c]).astype(BF16)

    for h in range(2):
        second_up[h].wait_recv()
        second_down[h].wait_recv()
    for copy in local:
        copy.wait()
    size = SIDE * part
    cut = size // 2
    rows_up, rows_down, rest_up, rest_down = [], [], [], []
    for h in range(2):
        start = row_start(h, outer_at[h])
        rows_up.append(pass_leaf(8 + h * 6, start, cut, near(h, 1, 0)))
        rows_down.append(pass_leaf(9 + h * 6, start + cut, size - cut, near(h, -1, 0)))
    for h in range(2):
        start = row_start(h, outer_at[h])
        rest_up.append(pass_leaf(10 + h * 6, start + cut, size - cut, near(h, 1, 0)))
        rest_down.append(pass_leaf(11 + h * 6, start, cut, near(h, -1, 0)))
    shared = [pass_leaf(20 + h * 4, row_start(h, outer_at[h]), size, sibling) for h in range(2)]
    ring_step(1)

    @pl.loop(0, count)
    def _(t):
        mixed = nn(shuffle, change_ref[t]).astype(BF16)
        for c in range(links):
            half_rows[t * links + c] = nn(mixed, leaf_blocks_ref[t, c]).astype(BF16)

    ring_step(2)
    ring_step(3)
    ring_step(4)
    last_up, last_down = [], []
    for h in range(2):
        rows_up[h].wait_recv()
        last_up.append(pass_leaf(12 + h * 6, row_start(h, outer_at[h] - 1), cut, near(h, 1, 0)))
        rows_down[h].wait_recv()
        last_down.append(
            pass_leaf(13 + h * 6, row_start(h, outer_at[h] + 1) + cut, size - cut, near(h, -1, 0))
        )
    ring_step(5)
    ring_step(6)
    for h in range(2):
        rest_up[h].wait_recv()
        shared.append(pass_leaf(21 + h * 4, row_start(h, outer_at[h] - 1), size, sibling))
        rest_down[h].wait_recv()
        shared.append(pass_leaf(22 + h * 4, row_start(h, outer_at[h] + 1), size, sibling))
    ring_step(7)

    blank = jnp.zeros((rank, 2 * rank), BF16)

    def couple(half_pair, distant):
        pair = jnp.concatenate([half_pair[:low], half_pair[low:]], axis=1)
        twice = jnp.concatenate(
            [
                jnp.concatenate([distant, blank], axis=1),
                jnp.concatenate([blank, distant], axis=1),
            ],
            axis=0,
        )
        return nt(pair, twice)

    def flatten(out, at, width):
        for q in range(low):
            rows = staged[pl.ds(q, width, stride=low), :]
            out[at, :, 2 * rank * q : 2 * rank * (q + 1)] = rows.astype(BF16)

    @pl.loop(0, parent_count)
    def _(p):
        for c in range(parent_links):
            index = parent_group_ref[p, c] * parent_count + parent_slot_ref[p, c]
            staged[low * c : low * (c + 1), :] = couple(
                parent_half_rows[p * parent_links + c], parents[index]
            )
        flatten(parent_out, p, parent_links)

    for h in range(2):
        last_up[h].wait_recv()
        last_down[h].wait_recv()
        shared.append(pass_leaf(23 + h * 4, row_start(h, outer_at[h] + 2), size, sibling))
    for copy in shared:
        copy.wait_recv()

    @pl.loop(0, count)
    def _(t):
        for c in range(links):
            place, slot = leaf_dev_ref[t, c], leaf_slot_ref[t, c]
            x, y, z = place // (2 * SIDE), place // 2 % SIDE, place % 2
            h = slot // part
            outer, inner = y + h * (x - y), x + h * (y - x)
            index = (((h * 2 + z) * SIDE + outer) * SIDE + inner) * part + slot - h * part
            staged[low * c : low * (c + 1), :] = couple(half_rows[t * links + c], leaves[index])
        flatten(leaf_out, t, links)

    for copy in started:
        copy.wait_send()


def shards(
    leaf_bases,
    leaf_transfers,
    leaf_blocks,
    leaf_partner_dev,
    leaf_partner_slot,
    parent_blocks,
    parent_partner_group,
    parent_partner_slot,
    leaf_start,
    parent_start,
):
    leaf_count, leaf_links = leaf_blocks.shape[:2]
    half_count, parent_links = parent_blocks.shape[:2]
    rank_new, rank_old = leaf_start.shape
    points = leaf_bases.shape[1]
    groups, members = lax.axis_size("grp"), lax.axis_size("sub")
    square = (rank_old, rank_old)
    block = (rank_new, rank_old)

    def shape(*sizes, dtype=F32):
        return jax.ShapeDtypeStruct(sizes, dtype)

    parent_weight, parent_sent = pl.pallas_call(
        parent_weight_kernel,
        out_shape=(shape(half_count, *square), shape(half_count, *square, dtype=BF16)),
        name="parent_weight",
    )(parent_blocks)
    other_weight = partner(parent_sent, "sub", 0)
    leaf_weight = pl.pallas_call(
        leaf_weight_kernel,
        out_shape=shape(leaf_count, *square),
        cost_estimate=pl.CostEstimate(
            flops=2 * leaf_count * leaf_links * rank_old**3, bytes_accessed=3 << 20, transcendentals=0
        ),
        name="leaf_weight",
    )(leaf_blocks)
    change, kept, sent = pl.pallas_call(
        leaf_kernel,
        out_shape=(
            shape(leaf_count, *block, dtype=BF16),
            shape(half_count, *block),
            shape(half_count, *block, dtype=BF16),
        ),
        scratch_shapes=[pltpu.VMEM((leaf_count, *block), F32)] * 2,
        name="leaf_rows",
    )(leaf_weight, parent_weight, other_weight, leaf_transfers, leaf_start)
    received = partner(sent, "sub", 0)
    parent_change = pl.pallas_call(
        parent_kernel,
        out_shape=shape(half_count, *block, dtype=BF16),
        scratch_shapes=[
            pltpu.VMEM((half_count, *block), F32),
            pltpu.VMEM((half_count, *block), F32),
            pltpu.VMEM((half_count, *square), F32),
        ],
        name="parent_rows",
    )(parent_weight, kept, received, parent_start)

    whole, scalars = pl.BlockSpec(memory_space=pltpu.VMEM), pl.BlockSpec(memory_space=pltpu.SMEM)
    return pl.pallas_call(
        functools.partial(couple_kernel, groups),
        out_shape=(
            shape(leaf_count, rank_new, points, dtype=BF16),
            shape(leaf_count, leaf_links, rank_new * rank_new, dtype=BF16),
            shape(half_count, parent_links, rank_new * rank_new, dtype=BF16),
        ),
        in_specs=[scalars] * 4 + [whole] * 5,
        out_specs=(whole,) * 3,
        scratch_shapes=[
            pltpu.VMEM((members * leaf_count, *block), BF16),
            pltpu.VMEM((groups * half_count, *block), BF16),
            pltpu.VMEM((leaf_count * leaf_links, *block), BF16),
            pltpu.VMEM((half_count * parent_links, *block), BF16),
            pltpu.VMEM((leaf_links * rank_new // 2, 2 * rank_new), F32),
            pltpu.SemaphoreType.DMA((3,)),
            pltpu.SemaphoreType.DMA((28,)),
            pltpu.SemaphoreType.DMA((28,)),
            pltpu.SemaphoreType.DMA((32,)),
            pltpu.SemaphoreType.DMA((32,)),
        ],
        compiler_params=pltpu.CompilerParams(collective_id=0, has_side_effects=True),
        name="couple",
    )(
        leaf_partner_dev, leaf_partner_slot, parent_partner_group, parent_partner_slot,
        change, parent_change, leaf_bases, leaf_blocks, parent_blocks,
    )


def solution(mesh):
    placed = (
        P(("grp", "sub"), None, None),
        P(("grp", "sub"), None, None),
        P(("grp", "sub"), None, None, None),
        P(("grp", "sub"), None),
        P(("grp", "sub"), None),
        P(("grp", "sub"), None, None, None),
        P(("grp", "sub"), None),
        P(("grp", "sub"), None),
        P(),
        P(),
    )
    return jax.shard_map(
        shards,
        mesh=mesh,
        in_specs=placed,
        out_specs=(
            P(("grp", "sub"), None, None),
            P(("grp", "sub"), None, None),
            P(("grp", "sub"), None, None),
        ),
        check_vma=False,
    )
```

time: 400 us -> 123 us (0.31)
  other arithmetic: 207 us -> 0 us
  waiting for transfers between devices: 128 us -> 0.01 us
  Pallas kernels: 0 us -> 102 us
  matrix products: 23.6 us -> 0 us
  between operations: 14.4 us -> 0.69 us
  local copies, waits for them, and re-layouts: 15 us -> 8.61 us
    another operation x12 -> x0, other arithmetic: 202 us -> none  [the longest x7 109 us: subspace(): factor = jnp.linalg.cholesky(cross_gram)]
    all_gather x2 -> x0, waiting for transfers between devices: 126 us -> none  [the longest x1 69.6 us: shards(): everyone = lax.all_gather(change, 'sub', axis=0, tiled=True)]
    pallas_call x0 -> x5, Pallas kernels: none -> 102 us  [the longest x1 49.1 us: shards(): pl.pallas_call(functools.partial(couple_kernel, groups), out_shape=(shape...]
    dot_general x17 -> x0, matrix products: 21.3 us -> none  [the longest x1 3.39 us: shards(): jnp.einsum('jcrl,jcsl->jcrs', leaf_midpoint, distant_site, preferred_elem...]
    unnamed x22 -> x21, local copies, waits for them, and re-layouts: 0.5 us -> 8.61 us
    gather x2 -> x0, local copies, waits for them, and re-layouts: 6.62 us -> none  [the longest x1 4.61 us: shards(): everyone[(leaf_partner_dev * leaf_count + leaf_partner_slot).reshape(-1)]]
    reshape x4 -> x0, local copies, waits for them, and re-layouts: 4.94 us -> none  [the longest x1 2.9 us: shards(): new_leaf_blocks.reshape(leaf_count, leaf_links, rank_new * rank_new)]
  transfers between devices with their start and end apart: 4 -> 2, of which waited for: 3 -> 0; matrix products, arithmetic and copies ran while one was open for 3% -> 2% of each run, Pallas kernels for 0% -> 4%
where the time goes in v1:
time: 123 us; the launch traced here: 122 us
  Pallas kernels  102 us (83%)
  starting transfers between devices  11 us (9%)
  local copies, waits for them, and re-layouts  8.61 us (7%)
    pallas_call x1, Pallas kernels, shards(): pl.pallas_call(functools.partial(couple_kernel, groups), out_shape=(shape...  49.1 us
    pallas_call x1, Pallas kernels, shards(): pl.pallas_call(leaf_kernel, out_shape=(shape(leaf_count, *block, dtype=BF...  25.4 us
    pallas_call x1, Pallas kernels, shards(): pl.pallas_call(parent_kernel, out_shape=shape(half_count, *block, dtype=B...  19.5 us
    ppermute x2, starting transfers between devices, partner(): return lax.ppermute(block, axis, route)  11 us
    unnamed x21, local copies, waits for them, and re-layouts  8.61 us
    pallas_call x1, Pallas kernels, shards(): pl.pallas_call(leaf_weight_kernel, out_shape=shape(leaf_count, *square),...  5.07 us
    pallas_call x1, Pallas kernels, shards(): pl.pallas_call(parent_weight_kernel, out_shape=(shape(half_count, *square...  3.08 us
  transfers between devices with their start and end apart: 2, of which 0 were waited for; matrix products, arithmetic and copies ran while one was open for 2% of the time, Pallas kernels for 4%

profile of v1, /device:TPU:1, one launch (start us, length us, event | category | flops | bytes accessed | tf_op | source)
XLA Modules:
  0.0 122.5 jit_solution(5038168038565705848)
XLA Ops:
  0.6 3.1 %parent_weight.1 = (f32[6,128,128]{2,1,0:T(8,128)}, bf16[6,128,128]{2,1,0:T(8,128)(2,1)}) custom-call(bf16[6,3,128,128]{3,2,1,0:T(8,128)(2,1)} %parent_blocks_ref.1), custom_call_target="tpu_custom_call" | custom-call | tf_op jit(solution)/shard_map/parent_weight/pallas_call | solution.py:417
  3.7 0.0 copy-start.5
  3.7 0.0 copy-start.6
  3.7 0.0 copy-start.3
  3.7 0.0 copy-start.4
  3.7 8.9 %collective-permute-start = (bf16[6,128,128]{2,1,0:T(8,128)(2,1)}, bf16[6,128,128]{2,1,0:T(8,128)(2,1)S(1)}, u32[]{:S(2)}, u32[]{:S(2)}) collective-permute-start(bf16[6,128,128]{2,1,0:T(8,128)(2,1)} %get-tuple-element.9), channel_id=1, source_target_pairs={{0,1},{1,0},{2,3},{3,2},{4,5},{5,4},{6,7},{7,6},{8,9},{9,8},{10,11... | collective-permute-start | bytes 589832 | tf_op jit(solution)/shard_map/ppermute | solution.py:36
  12.6 5.1 %leaf_weight.1.weight_ref = f32[12,128,128]{2,1,0:T(8,128)} custom-call(bf16[12,6,128,128]{3,2,1,0:T(8,128)(2,1)} %leaf_blocks_ref.1), custom_call_target="tpu_custom_call" | custom-call | flops 301989888 | bytes 3145728 | tf_op jit(solution)/shard_map/leaf_weight/pallas_call | solution.py:423
  17.7 0.0 collective-permute-done.other_ref
  17.7 0.0 copy-start
  17.7 0.7 copy-done
  18.4 25.4 %leaf_rows.1 = (bf16[12,64,128]{2,1,0:T(8,128)(2,1)}, f32[6,64,128]{2,1,0:T(8,128)}, bf16[6,64,128]{2,1,0:T(8,128)(2,1)}) custom-call(f32[12,128,128]{2,1,0:T(8,128)} %leaf_weight.1.weight_ref, f32[6,128,128]{2,1,0:T(8,128)} %get-tuple-element.8.own_ref.weight_ref, bf16[6,128,128]{2,1,0:T(8,128)(2,1)} %copy-done, bf16[12,128,128]{2,1,0:T(8,128)(2,1)} %transfers_ref.1, ...), custom_call_target="tpu_custom_call" | custom-call | tf_op jit(solution)/shard_map/leaf_rows/pallas_call | solution.py:431
  43.8 2.1 %collective-permute-start.1 = (bf16[6,64,128]{2,1,0:T(8,128)(2,1)}, bf16[6,64,128]{2,1,0:T(8,128)(2,1)S(1)}, u32[]{:S(2)}, u32[]{:S(2)}) collective-permute-start(bf16[6,64,128]{2,1,0:T(8,128)(2,1)} %get-tuple-element.12), channel_id=1, source_target_pairs={{0,1},{1,0},{2,3},{3,2},{4,5},{5,4},{6,7},{7,6},{8,9},{9,8},{10,11... | collective-permute-start | bytes 294920 | tf_op jit(solution)/shard_map/ppermute | solution.py:36
  45.9 0.0 copy-done.5
  45.9 0.7 copy.15.parent_group_ref
  46.6 0.0 copy-done.6
  46.6 0.7 copy.16.parent_slot_ref
  47.2 0.0 copy-done.3
  47.2 0.7 copy.13.leaf_dev_ref
  47.9 0.0 copy-done.4
  47.9 0.7 copy.14.leaf_slot_ref
  48.6 0.0 collective-permute-done.1.received_ref
  48.6 0.0 copy-start.2
  48.6 0.6 copy-done.2
  49.3 19.5 %parent_rows.1.parent_change_ref = bf16[6,64,128]{2,1,0:T(8,128)(2,1)} custom-call(f32[6,128,128]{2,1,0:T(8,128)} %get-tuple-element.8.own_ref.weight_ref, f32[6,64,128]{2,1,0:T(8,128)} %get-tuple-element.11.kept_ref, bf16[6,64,128]{2,1,0:T(8,128)(2,1)} %copy-done.2, f32[64,128]{1,0:T(8,128)} %start_ref.3), custom_call_target="tpu_custom_call" | custom-call | tf_op jit(solution)/shard_map/parent_rows/pallas_call | solution.py:442
  68.8 49.1 %couple.1 = (bf16[12,64,256]{2,1,0:T(8,128)(2,1)}, bf16[12,6,4096]{2,1,0:T(8,128)(2,1)}, bf16[6,3,4096]{2,1,0:T(4,128)(2,1)}) custom-call(s32[12,6]{1,0:T(8,128)} %copy.13.leaf_dev_ref, s32[12,6]{1,0:T(8,128)} %copy.14.leaf_slot_ref, s32[6,3]{1,0:T(8,128)} %copy.15.parent_group_ref, s32[6,3]{1,0:T(8,128)} %copy.16.parent_slot_ref, ...), custom_call_target="tpu_custom_call" | custom-call | tf_op jit(solution)/shard_map/couple/pallas_call | solution.py:454
  117.9 0.0 copy-start.1
  117.9 1.8 %copy.20 = bf16[12,64,256]{2,1,0:T(8,128)(2,1)} copy(bf16[12,64,256]{2,1,0:T(8,128)(2,1)} %get-tuple-element.16) | data formatting | bytes 786432
  119.7 2.1 %copy.21 = bf16[12,6,4096]{2,1,0:T(8,128)(2,1)} copy(bf16[12,6,4096]{2,1,0:T(8,128)(2,1)} %get-tuple-element.17) | data formatting | bytes 1179648
  121.8 0.0 copy-done.1
  121.8 0.7 copy.22
Async XLA Ops:
  3.7 42.2 %copy-start.5 = (s32[6,3]{0,1:T(4,128)S(1)}, s32[6,3]{0,1:T(4,128)}, u32[]{:S(2)}) copy-start(s32[6,3]{0,1:T(4,128)} %param.16) | copy-start | bytes 220
  3.7 42.9 %copy-start.6 = (s32[6,3]{0,1:T(4,128)S(1)}, s32[6,3]{0,1:T(4,128)}, u32[]{:S(2)}) copy-start(s32[6,3]{0,1:T(4,128)} %param.17) | copy-start | bytes 220
  3.7 43.5 %copy-start.3 = (s32[12,6]{0,1:T(8,128)S(1)}, s32[12,6]{0,1:T(8,128)}, u32[]{:S(2)}) copy-start(s32[12,6]{0,1:T(8,128)} %param.13) | copy-start | bytes 868
  3.7 44.2 %copy-start.4 = (s32[12,6]{0,1:T(8,128)S(1)}, s32[12,6]{0,1:T(8,128)}, u32[]{:S(2)}) copy-start(s32[12,6]{0,1:T(8,128)} %param.14) | copy-start | bytes 868
  3.7 14.0 %collective-permute-start = (bf16[6,128,128]{2,1,0:T(8,128)(2,1)}, bf16[6,128,128]{2,1,0:T(8,128)(2,1)S(1)}, u32[]{:S(2)}, u32[]{:S(2)}) collective-permute-start(bf16[6,128,128]{2,1,0:T(8,128)(2,1)} %get-tuple-element.9), channel_id=1, source_target_pairs={{0,1},{1,0},{2,3},{3,2},{4,5},{5,4},{6,7},{7,6},{8,9},{9,8},{10,11... | collective-permute-start | bytes 589832 | tf_op jit(solution)/shard_map/ppermute | solution.py:36
  17.7 0.7 copy-start
  43.8 4.8 %collective-permute-start.1 = (bf16[6,64,128]{2,1,0:T(8,128)(2,1)}, bf16[6,64,128]{2,1,0:T(8,128)(2,1)S(1)}, u32[]{:S(2)}, u32[]{:S(2)}) collective-permute-start(bf16[6,64,128]{2,1,0:T(8,128)(2,1)} %get-tuple-element.12), channel_id=1, source_target_pairs={{0,1},{1,0},{2,3},{3,2},{4,5},{5,4},{6,7},{7,6},{8,9},{9,8},{10,11... | collective-permute-start | bytes 294920 | tf_op jit(solution)/shard_map/ppermute | solution.py:36
  48.6 0.6 copy-start.2
  117.9 3.9 %copy-start.1 = (bf16[6,3,4096]{2,1,0:T(4,128)(2,1)S(1)}, bf16[6,3,4096]{2,1,0:T(4,128)(2,1)}, u32[]{:S(2)}) copy-start(bf16[6,3,4096]{2,1,0:T(4,128)(2,1)} %get-tuple-element.18) | copy-start | bytes 442372

commit v2 on v0

v2 whole, which is shorter than its diff:
```python
import functools

import jax
import jax.numpy as jnp
from jax import lax
from jax.experimental import pallas as pl
from jax.experimental.pallas import tpu as pltpu
from jax.sharding import PartitionSpec as P

MESH = pl.DeviceIdType.MESH
F32 = jnp.float32
BF16 = jnp.bfloat16
SIDE = 4


def nt(left, right):
    return lax.dot_general(left, right, (((1,), (1,)), ((), ())), preferred_element_type=F32)


def nn(left, right):
    return lax.dot_general(left, right, (((1,), (0,)), ((), ())), preferred_element_type=F32)


def beside(*parts):
    return jnp.concatenate(parts, axis=1)


def above(*parts):
    return jnp.concatenate(parts, axis=0)


def split(values):
    high = values.astype(BF16)
    return high, (values - high.astype(F32)).astype(BF16)


def fold(values):
    width = values.shape[1] // 2
    return values[:, :width] + values[:, width:]


def product(left, right):
    wide = beside(*right)
    return fold(nn(beside(*left), above(wide, wide)))


def product_t(left, right):
    high, low = right
    return fold(nt(beside(*left), above(beside(high, high), beside(low, low))))


def panel(tiles, at):
    full = tiles[0].shape
    rows, width = full[1:]
    half = width // 2
    flat = (full[0] * rows, width)
    place = lax.broadcasted_iota(jnp.int32, full, 1)
    inside = lax.broadcasted_iota(jnp.int32, full, 2) % half - at * rows
    owned = (inside >= 0) & (inside < rows)
    base = lax.broadcasted_iota(jnp.int32, flat, 1) // half * half + at * rows

    def column(values, j):
        picked = jnp.take_along_axis(values.reshape(flat), base + j, axis=1, mode="promise_in_bounds")
        return picked.reshape(full)

    def line(values, j):
        return jnp.broadcast_to(values[:, j : j + 1, :], full)

    tile = tiles[at]
    columns = [column(tile, j) for j in range(rows)]
    tile = jnp.where(owned, jnp.where(inside == place, 1.0, 0.0), tile)
    scale = jnp.zeros(full, F32)
    recip = jnp.zeros(full, F32)
    for k in range(rows):
        inverse = 1.0 / columns[k]
        scale = jnp.where(place == k, lax.rsqrt(columns[k]), scale)
        recip = jnp.where(place == k, inverse, recip)
        if k < rows - 1:
            factor = jnp.where(place > k, columns[k] * line(inverse, k), 0.0)
            for j in range(k + 1, rows):
                columns[j] = columns[j] - factor * line(columns[j], k)
            tile = tile - factor * line(tile, k)
    tiles[at] = jnp.where(inside < rows, tile * scale, 0.0)
    if at + 1 == len(tiles):
        return
    solved = tile * recip
    for k in range(rows - 1, 0, -1):
        solved = solved - jnp.where(place < k, columns[k] * recip, 0.0) * line(solved, k)
    lines = [line(solved, j) for j in range(rows)]
    for i in range(at + 1, len(tiles)):
        old = tiles[i]
        parts = [column(old, j) * lines[j] for j in range(rows)]
        while len(parts) > 1:
            parts = [left + right for left, right in zip(parts[::2], parts[1::2])]
        tiles[i] = jnp.where(owned, 0.0, old) - parts[0]


def eliminate(grams):
    tiles = [grams[:, 8 * i : 8 * i + 8, :] for i in range(grams.shape[1] // 8)]
    for at in range(len(tiles)):
        panel(tiles, at)
    return jnp.concatenate(tiles, axis=1)


def image_of(start, weight):
    terms = split(weight)
    return split(product(split(product(start, terms)), terms))


def diagonal(first, second):
    blank = jnp.zeros_like(first)
    return above(beside(first, blank), beside(blank, second))


def gram_pair(first, second):
    rows = first[0].shape[0]
    left = above(beside(first[0], second[0]), beside(first[1], second[1]))
    right = above(diagonal(first[0], second[0]), diagonal(first[1], second[1]))
    both = fold(nt(left, right))
    return both[:rows] + both[rows:]


def rows_pair(inverses, first, second):
    left = beside(*split(inverses))
    both = 0.0
    for part in range(2):
        block = diagonal(first[part], second[part])
        both = both + nn(left, above(block, block))
    width = both.shape[1] // 2
    return both[:, :width], both[:, width:]


def kernel(
    groups,
    leaf_dev_in, leaf_slot_in, parent_group_in, parent_slot_in,
    leaf_start_ref, parent_start_ref, bases_in, transfers_in, leaf_blocks_in, parent_blocks_in,
    bases_out, leaf_out, parent_out,
    leaf_dev_ref, leaf_slot_ref, parent_group_ref, parent_slot_ref,
    bases_ref, transfers_ref, leaf_blocks_ref, parent_blocks_ref,
    leaves, parents, change, parent_change, half_rows, parent_half_rows, staged,
    weight_high, weight_low, other_weight, kept, sent, received, stacked_high, stacked_low,
    image_high, image_low, grams, parent_image_high, parent_image_low, parent_grams,
    load_sem, pair_send, pair_recv, leaf_send, leaf_recv, ring_send, ring_recv,
):
    count, links = leaf_blocks_ref.shape[:2]
    parent_count, parent_links = parent_blocks_ref.shape[:2]
    rank = change.shape[1]
    part = count // 2
    chunk = parent_count // 2
    sub, grp = lax.axis_index("sub"), lax.axis_index("grp")
    across, along, core = sub // (2 * SIDE), (sub // 2) % SIDE, sub % 2
    member = core

    def site(x, y, c):
        return ((x + SIDE) % SIDE * SIDE + (y + SIDE) % SIDE) * 2 + c

    def near(h, outer, inner):
        if h == 0:
            return site(across + inner, along + outer, core)
        return site(across + outer, along + inner, core)

    outer_at = (along, across)
    inner_at = (across, along)

    def row_start(h, outer):
        return ((h * 2 + core) * SIDE + (outer + SIDE) % SIDE) * SIDE * part

    def block_start(h, outer, inner):
        return row_start(h, outer) + (inner + SIDE) % SIDE * part

    up, down = (grp + 1) % groups, (grp + groups - 1) % groups
    sibling = site(across, along, 1 - core)

    barrier = pltpu.get_barrier_semaphore()
    for target in (near(0, 0, 1), near(0, 0, -1), near(0, 1, 0), near(0, -1, 0), sibling):
        pl.semaphore_signal(barrier, inc=1, device_id={"sub": target}, device_id_type=MESH)
    for target in (up, down):
        pl.semaphore_signal(barrier, inc=1, device_id={"grp": target}, device_id_type=MESH)

    loads = [
        pltpu.make_async_copy(src, dst, load_sem.at[n])
        for n, (src, dst) in enumerate(
            (
                (parent_blocks_in, parent_blocks_ref),
                (leaf_blocks_in, leaf_blocks_ref),
                (transfers_in, transfers_ref),
                (bases_in, bases_ref),
                (leaf_dev_in, leaf_dev_ref),
                (leaf_slot_in, leaf_slot_ref),
                (parent_group_in, parent_group_ref),
                (parent_slot_in, parent_slot_ref),
            )
        )
    ]
    for copy in loads:
        copy.start()

    started = []

    def send_pair(number, src, dst):
        copy = pltpu.make_async_remote_copy(
            src_ref=src,
            dst_ref=dst,
            send_sem=pair_send.at[number],
            recv_sem=pair_recv.at[number],
            device_id={"sub": sibling},
            device_id_type=MESH,
        )
        copy.start()
        started.append(copy)
        return copy

    def send_leaf(number, src, start, size, target):
        copy = pltpu.make_async_remote_copy(
            src_ref=src,
            dst_ref=leaves.at[pl.ds(start, size)],
            send_sem=leaf_send.at[number],
            recv_sem=leaf_recv.at[number],
            device_id={"sub": target},
            device_id_type=MESH,
        )
        copy.start()
        started.append(copy)
        return copy

    def pass_leaf(number, start, size, target):
        return send_leaf(number, leaves.at[pl.ds(start, size)], start, size, target)

    def send_parent(way, step, piece):
        number = (way * (groups // 2) + step) * 2 + piece
        origin = (grp - step + groups) % groups if way == 0 else (grp + step) % groups
        at = origin * parent_count + piece * chunk
        src = parent_change.at[pl.ds(piece * chunk, chunk)] if step == 0 else parents.at[pl.ds(at, chunk)]
        copy = pltpu.make_async_remote_copy(
            src_ref=src,
            dst_ref=parents.at[pl.ds(at, chunk)],
            send_sem=ring_send.at[number],
            recv_sem=ring_recv.at[number],
            device_id={"grp": up if way == 0 else down},
            device_id_type=MESH,
        )
        copy.start()
        started.append(copy)
        return copy

    loads[0].wait()

    @pl.loop(0, parent_count, unroll=3)
    def _(p):
        total = nt(parent_blocks_ref[p, 0], parent_blocks_ref[p, 0])
        for c in range(1, parent_links):
            total = total + nt(parent_blocks_ref[p, c], parent_blocks_ref[p, c])
        weight_high[p], weight_low[p] = split(total)

    loads[1].wait()
    loads[2].wait()
    pl.semaphore_wait(barrier, 7)
    other_sent = send_pair(0, weight_high, other_weight)

    start = split(leaf_start_ref[...])

    def leaf_image(which, p, high, low):
        t = (member + which * (1 - 2 * member)) * part + p
        weight = None
        for c in range(0, links, 2):
            pair = beside(leaf_blocks_ref[t, c], leaf_blocks_ref[t, c + 1])
            weight = nt(pair, pair) if weight is None else weight + nt(pair, pair)
        transfer = transfers_ref[t]
        twice = beside(transfer, transfer)
        carried = nn(transfer, high) if low is None else nn(twice, above(high, low))
        weight = weight + nt(beside(*split(carried)), twice)
        image_high[which * part + p], image_low[which * part + p] = image_of(start, weight)

    @pl.loop(0, part, unroll=3)
    def _(p):
        leaf_image(0, p, weight_high[p], weight_low[p])

    other_sent.wait_recv()

    @pl.loop(0, part, unroll=3)
    def _(p):
        leaf_image(1, p, other_weight[p], None)

    def leaf_terms(which, p):
        return image_high[which * part + p], image_low[which * part + p]

    @pl.loop(0, part, unroll=3)
    def _(p):
        grams[p] = gram_pair(leaf_terms(0, p), leaf_terms(1, p))

    grams[...] = eliminate(grams[...])

    own_start = [block_start(h, outer_at[h], inner_at[h]) for h in range(2)]

    @pl.loop(0, part, unroll=3)
    def _(p):
        both = rows_pair(grams[p], leaf_terms(0, p), leaf_terms(1, p))
        for which in range(2):
            h = member + which * (1 - 2 * member)
            t = h * part + p
            rows = both[which].astype(BF16)
            change[t] = rows
            leaves[own_start[0] + h * (own_start[1] - own_start[0]) + p] = rows
            projected = nn(rows, transfers_ref[t])
            if which == 0:
                kept[p] = projected
            else:
                sent[p] = projected.astype(BF16)

    rows_sent = send_pair(1, sent, received)
    inner_up, inner_down = [], []
    for h in range(2):
        own = change.at[pl.ds(h * part, part)]
        inner_up.append(send_leaf(h * 2, own, own_start[h], part, near(h, 0, 1)))
        inner_down.append(send_leaf(h * 2 + 1, own, own_start[h], part, near(h, 0, -1)))

    loads[3].wait()

    @pl.loop(0, count, unroll=3)
    def _(t):
        bases_out[t] = nt(change[t], bases_ref[t]).astype(BF16)

    rows_sent.wait_recv()
    parent_start = split(parent_start_ref[...])
    first = member == 0

    @pl.loop(0, parent_count, unroll=3)
    def _(p):
        mine, other = kept[p], received[p].astype(F32)
        stacked = split(above(jnp.where(first, mine, other), jnp.where(first, other, mine)))
        stacked_high[p], stacked_low[p] = stacked
        left = product(stacked, (weight_high[p], weight_low[p]))
        gram = product_t(split(left), stacked)
        parent_image_high[p], parent_image_low[p] = image_of(parent_start, gram)

    def parent_terms(p):
        return parent_image_high[p], parent_image_low[p]

    @pl.loop(0, chunk, unroll=3)
    def _(p):
        parent_grams[p] = gram_pair(parent_terms(p), parent_terms(p + chunk))

    for h in range(2):
        inner_up[h].wait_recv()
        inner_down[h].wait_recv()
    second_up, second_down = [], []
    cut = part // 2
    for h in range(2):
        outer, inner = outer_at[h], inner_at[h]
        second_up.append(
            pass_leaf(4 + h * 2, block_start(h, outer, inner - 1), cut, near(h, 0, 1))
        )
        second_down.append(
            pass_leaf(5 + h * 2, block_start(h, outer, inner + 1) + cut, part - cut, near(h, 0, -1))
        )

    parent_grams[...] = eliminate(parent_grams[...])

    @pl.loop(0, chunk, unroll=3)
    def _(p):
        both = rows_pair(parent_grams[p], parent_terms(p), parent_terms(p + chunk))
        for which in range(2):
            q = p + which * chunk
            rows = product(split(both[which]), (stacked_high[q], stacked_low[q])).astype(BF16)
            parent_change[q] = rows
            parents[grp * parent_count + q] = rows

    ring = {}
    for piece in range(2):
        for way in range(2):
            ring[way, 0, piece] = send_parent(way, 0, piece)

    def ring_step(step):
        for piece in range(2):
            for way in range(2):
                if (way, step, piece) not in ring:
                    continue
                ring[way, step, piece].wait_recv()
                if step < groups // 2 - 2 or (step == groups // 2 - 2 and way == piece):
                    ring[way, step + 1, piece] = send_parent(way, step + 1, piece)

    for h in range(2):
        second_up[h].wait_recv()
        second_down[h].wait_recv()
    size = SIDE * part
    cut = size // 2
    rows_up, rows_down, rest_up, rest_down = [], [], [], []
    for h in range(2):
        at = row_start(h, outer_at[h])
        rows_up.append(pass_leaf(8 + h * 6, at, cut, near(h, 1, 0)))
        rows_down.append(pass_leaf(9 + h * 6, at + cut, size - cut, near(h, -1, 0)))
    for h in range(2):
        at = row_start(h, outer_at[h])
        rest_up.append(pass_leaf(10 + h * 6, at + cut, size - cut, near(h, 1, 0)))
        rest_down.append(pass_leaf(11 + h * 6, at, cut, near(h, -1, 0)))
    shared = [pass_leaf(20 + h * 4, row_start(h, outer_at[h]), size, sibling) for h in range(2)]

    row = lax.broadcasted_iota(jnp.int32, (rank, rank), 0)
    column = lax.broadcasted_iota(jnp.int32, (rank, rank), 1)
    low = rank // 2
    order = jnp.where(row < low, 2 * row, 2 * (row - low) + 1)
    shuffle = jnp.where(column == order, 1.0, 0.0).astype(BF16)

    @pl.loop(0, parent_count, unroll=3)
    def _(p):
        mixed = nn(shuffle, parent_change[p]).astype(BF16)
        for c in range(parent_links):
            parent_half_rows[p * parent_links + c] = nn(mixed, parent_blocks_ref[p, c]).astype(BF16)

    def leaf_halves(begin, end):
        @pl.loop(begin, end, unroll=3)
        def _(t):
            mixed = nn(shuffle, change[t]).astype(BF16)
            for c in range(links):
                half_rows[t * links + c] = nn(mixed, leaf_blocks_ref[t, c]).astype(BF16)

    ring_step(0)
    leaf_halves(0, 3)
    ring_step(1)
    leaf_halves(3, 6)
    ring_step(2)
    leaf_halves(6, 9)
    ring_step(3)
    leaf_halves(9, 12)
    last_up, last_down = [], []
    for h in range(2):
        rows_up[h].wait_recv()
        last_up.append(pass_leaf(12 + h * 6, row_start(h, outer_at[h] - 1), cut, near(h, 1, 0)))
        rows_down[h].wait_recv()
        last_down.append(
            pass_leaf(13 + h * 6, row_start(h, outer_at[h] + 1) + cut, size - cut, near(h, -1, 0))
        )
    ring_step(4)
    for h in range(2):
        rest_up[h].wait_recv()
        shared.append(pass_leaf(21 + h * 4, row_start(h, outer_at[h] - 1), size, sibling))
        rest_down[h].wait_recv()
        shared.append(pass_leaf(22 + h * 4, row_start(h, outer_at[h] + 1), size, sibling))
    ring_step(5)
    for h in range(2):
        last_up[h].wait_recv()
        last_down[h].wait_recv()
        shared.append(pass_leaf(23 + h * 4, row_start(h, outer_at[h] + 2), size, sibling))
    ring_step(6)
    for copy in shared:
        copy.wait_recv()
    for copy in loads[4:]:
        copy.wait()

    def couple(half_pair, distant):
        return nt(beside(half_pair[:low], half_pair[low:]), diagonal(distant, distant))

    def flatten(out, at, slot, width):
        for q in range(low):
            rows = staged[slot, pl.ds(q, width, stride=low), :]
            out[at, :, 2 * rank * q : 2 * rank * (q + 1)] = rows.astype(BF16)

    @pl.loop(0, count // 2)
    def _(pair):
        for slot in range(2):
            t = pair * 2 + slot
            for c in range(links):
                place, at = leaf_dev_ref[c, t], leaf_slot_ref[c, t]
                x, y, z = place // (2 * SIDE), place // 2 % SIDE, place % 2
                h = at // part
                outer, inner = y + h * (x - y), x + h * (y - x)
                index = (((h * 2 + z) * SIDE + outer) * SIDE + inner) * part + at - h * part
                staged[slot, low * c : low * (c + 1), :] = couple(half_rows[t * links + c], leaves[index])
        for slot in range(2):
            flatten(leaf_out, pair * 2 + slot, slot, links)

    ring_step(7)

    @pl.loop(0, parent_count // 2)
    def _(pair):
        for slot in range(2):
            p = pair * 2 + slot
            for c in range(parent_links):
                index = parent_group_ref[c, p] * parent_count + parent_slot_ref[c, p]
                staged[slot, low * c : low * (c + 1), :] = couple(
                    parent_half_rows[p * parent_links + c], parents[index]
                )
        for slot in range(2):
            flatten(parent_out, pair * 2 + slot, slot, parent_links)

    for copy in started:
        copy.wait_send()


def shards(
    leaf_bases,
    leaf_transfers,
    leaf_blocks,
    leaf_partner_dev,
    leaf_partner_slot,
    parent_blocks,
    parent_partner_group,
    parent_partner_slot,
    leaf_start,
    parent_start,
):
    leaf_count, leaf_links = leaf_blocks.shape[:2]
    half_count, parent_links = parent_blocks.shape[:2]
    rank_new, rank_old = leaf_start.shape
    points = leaf_bases.shape[1]
    groups, members = lax.axis_size("grp"), lax.axis_size("sub")
    square = (rank_old, rank_old)
    block = (rank_new, rank_old)
    paired = (rank_new, 2 * rank_new)

    def shape(*sizes):
        return jax.ShapeDtypeStruct(sizes, BF16)

    def room(*sizes, dtype=BF16):
        return pltpu.VMEM(sizes, dtype)

    whole, outside = pl.BlockSpec(memory_space=pltpu.VMEM), pl.BlockSpec(memory_space=pl.ANY)
    indices = (leaf_partner_dev.T, leaf_partner_slot.T, parent_partner_group.T, parent_partner_slot.T)
    streams = (leaf_bases, leaf_transfers, leaf_blocks, parent_blocks)
    transfers = (2, 28, 4 * groups // 2)
    return pl.pallas_call(
        functools.partial(kernel, groups),
        out_shape=(
            shape(leaf_count, rank_new, points),
            shape(leaf_count, leaf_links, rank_new * rank_new),
            shape(half_count, parent_links, rank_new * rank_new),
        ),
        in_specs=[outside] * 4 + [whole] * 2 + [outside] * 4,
        out_specs=(whole,) * 3,
        scratch_shapes=[pltpu.SMEM(values.shape, jnp.int32) for values in indices]
        + [room(*values.shape) for values in streams]
        + [
            room(members * leaf_count, *block),
            room(groups * half_count, *block),
            room(leaf_count, *block),
            room(half_count, *block),
            room(leaf_count * leaf_links, *block),
            room(half_count * parent_links, *block),
            room(2, leaf_links * rank_new // 2, 2 * rank_new, dtype=F32),
            room(half_count, *square),
            room(half_count, *square),
            room(half_count, *square),
            room(half_count, *block, dtype=F32),
            room(half_count, *block),
            room(half_count, *block),
            room(half_count, *square),
            room(half_count, *square),
            room(leaf_count, *block),
            room(leaf_count, *block),
            room(leaf_count // 2, *paired, dtype=F32),
            room(half_count, *block),
            room(half_count, *block),
            room(half_count // 2, *paired, dtype=F32),
            pltpu.SemaphoreType.DMA((8,)),
        ]
        + [pltpu.SemaphoreType.DMA((number,)) for number in transfers for _ in range(2)],
        compiler_params=pltpu.CompilerParams(collective_id=0, has_side_effects=True),
        name="recompress",
    )(*indices, leaf_start, parent_start, *streams)


def solution(mesh):
    placed = (
        P(("grp", "sub"), None, None),
        P(("grp", "sub"), None, None),
        P(("grp", "sub"), None, None, None),
        P(("grp", "sub"), None),
        P(("grp", "sub"), None),
        P(("grp", "sub"), None, None, None),
        P(("grp", "sub"), None),
        P(("grp", "sub"), None),
        P(),
        P(),
    )
    return jax.shard_map(
        shards,
        mesh=mesh,
        in_specs=placed,
        out_specs=(
            P(("grp", "sub"), None, None),
            P(("grp", "sub"), None, None),
            P(("grp", "sub"), None, None),
        ),
        check_vma=False,
    )
```

time: 400 us -> 69.1 us (0.17)
  other arithmetic: 207 us -> 0 us
  waiting for transfers between devices: 128 us -> 0 us
  Pallas kernels: 0 us -> 63.7 us
  matrix products: 23.6 us -> 0 us
  between operations: 14.4 us -> 0.65 us
  starting transfers between devices: 11 us -> 0 us
  local copies, waits for them, and re-layouts: 15 us -> 4.55 us
    another operation x12 -> x0, other arithmetic: 202 us -> none  [the longest x7 109 us: subspace(): factor = jnp.linalg.cholesky(cross_gram)]
    all_gather x2 -> x0, waiting for transfers between devices: 126 us -> none  [the longest x1 69.6 us: shards(): everyone = lax.all_gather(change, 'sub', axis=0, tiled=True)]
    pallas_call x0 -> x1, Pallas kernels: none -> 63.7 us  [shards(): pl.pallas_call(functools.partial(kernel, groups), out_shape=(shape(leaf_c...]
    dot_general x17 -> x0, matrix products: 21.3 us -> none  [the longest x1 3.39 us: shards(): jnp.einsum('jcrl,jcsl->jcrs', leaf_midpoint, distant_site, preferred_elem...]
    ppermute x2 -> x0, starting transfers between devices: 10.9 us -> none  [partner(): return lax.ppermute(block, axis, route)]
    gather x2 -> x0, local copies, waits for them, and re-layouts: 6.62 us -> none  [the longest x1 4.61 us: shards(): everyone[(leaf_partner_dev * leaf_count + leaf_partner_slot).reshape(-1)]]
    reshape x4 -> x0, local copies, waits for them, and re-layouts: 4.94 us -> none  [the longest x1 2.9 us: shards(): new_leaf_blocks.reshape(leaf_count, leaf_links, rank_new * rank_new)]
    unnamed x22 -> x5, local copies, waits for them, and re-layouts: 0.5 us -> 4.55 us
  transfers between devices with their start and end apart: 4 -> 0, of which waited for: 3 -> 0; matrix products, arithmetic and copies ran while one was open for 3% -> 0% of each run, Pallas kernels for 0% -> 0%
where the time goes in v2:
time: 69.1 us; the launch traced here: 68.9 us
  Pallas kernels  63.7 us (92%)
  local copies, waits for them, and re-layouts  4.55 us (7%)
    pallas_call x1, Pallas kernels, shards(): pl.pallas_call(functools.partial(kernel, groups), out_shape=(shape(leaf_c...  63.7 us
    unnamed x5, local copies, waits for them, and re-layouts  4.55 us

profile of v2, /device:TPU:1, one launch (start us, length us, event | category | flops | bytes accessed | tf_op | source)
XLA Modules:
  0.0 68.9 jit_solution(716641033899984602)
XLA Ops:
  0.6 63.7 %recompress.1 = (bf16[12,64,256]{2,1,0:T(8,128)(2,1)}, bf16[12,6,4096]{2,1,0:T(8,128)(2,1)}, bf16[6,3,4096]{2,1,0:T(4,128)(2,1)}) custom-call(s32[6,12]{1,0:T(8,128)} %bitcast.4, s32[6,12]{1,0:T(8,128)} %bitcast.5, s32[3,6]{1,0:T(4,128)} %bitcast.6, s32[3,6]{1,0:T(4,128)} %bitcast.7, f32[64,128]{1,0:T(8,128)} %leaf_start_ref.1, f32[64,128]{1,0:T(8,128)} %parent_start_ref.1, ...), custom_call_target="tpu_custom_call" | custom-call | tf_op jit(solution)/shard_map/recompress/pallas_call | solution.py:521
  64.3 0.0 copy-start
  64.3 1.8 %copy.16 = bf16[12,64,256]{2,1,0:T(8,128)(2,1)} copy(bf16[12,64,256]{2,1,0:T(8,128)(2,1)} %get-tuple-element.6) | data formatting | bytes 786432
  66.1 2.1 %copy.17 = bf16[12,6,4096]{2,1,0:T(8,128)(2,1)} copy(bf16[12,6,4096]{2,1,0:T(8,128)(2,1)} %get-tuple-element.7) | data formatting | bytes 1179648
  68.2 0.0 copy-done
  68.2 0.7 copy.18
Async XLA Ops:
  64.3 3.9 %copy-start = (bf16[6,3,4096]{2,1,0:T(4,128)(2,1)S(1)}, bf16[6,3,4096]{2,1,0:T(4,128)(2,1)}, u32[]{:S(2)}) copy-start(bf16[6,3,4096]{2,1,0:T(4,128)(2,1)} %get-tuple-element.8) | copy-start | bytes 442372

commit v3 on v2

--- a/solution.py
+++ b/solution.py
@@ -509,7 +509,7 @@
     paired = (rank_new, 2 * rank_new)
 
     def shape(*sizes):
-        return jax.ShapeDtypeStruct(sizes, BF16)
+        return pltpu.VMEM(sizes, BF16)
 
     def room(*sizes, dtype=BF16):
         return pltpu.VMEM(sizes, dtype)

time: 69.1 us -> 65.7 us (0.951)
  local copies, waits for them, and re-layouts: 4.55 us -> 2.3 us
  Pallas kernels: 63.7 us -> 62.6 us
    unnamed x5 -> x3, local copies, waits for them, and re-layouts: 4.55 us -> 2.3 us
    pallas_call x1, Pallas kernels: 63.7 us -> 62.6 us  [shards(): pl.pallas_call(functools.partial(kernel, groups), out_shape=(shape(leaf_c...]
where the time goes in v3:
time: 65.7 us; the launch traced here: 65.5 us
  Pallas kernels  62.6 us (95%)
  local copies, waits for them, and re-layouts  2.3 us (4%)
    pallas_call x1, Pallas kernels, shards(): pl.pallas_call(functools.partial(kernel, groups), out_shape=(shape(leaf_c...  62.6 us
    unnamed x3, local copies, waits for them, and re-layouts  2.3 us

profile of v3, /device:TPU:1, one launch (start us, length us, event | category | flops | bytes accessed | tf_op | source)
XLA Modules:
  0.0 65.5 jit_solution(12063098286031980657)
XLA Ops:
  0.6 62.6 %recompress.1 = (bf16[12,64,256]{2,1,0:T(8,128)(2,1)S(1)}, bf16[12,6,4096]{2,1,0:T(8,128)(2,1)S(1)}, bf16[6,3,4096]{2,1,0:T(4,128)(2,1)S(1)}) custom-call(s32[6,12]{1,0:T(8,128)} %bitcast.4, s32[6,12]{1,0:T(8,128)} %bitcast.5, s32[3,6]{1,0:T(4,128)} %bitcast.6, s32[3,6]{1,0:T(4,128)} %bitcast.7, f32[64,128]{1,0:T(8,128)} %leaf_start_ref.1, ...), custom_call_target="tpu_custom_call" | custom-call | tf_op jit(solution)/shard_map/recompress/pallas_call | solution.py:521
  63.2 0.7 %copy.16 = bf16[12,64,256]{2,1,0:T(8,128)(2,1)} copy(bf16[12,64,256]{2,1,0:T(8,128)(2,1)S(1)} %get-tuple-element.3) | data formatting | bytes 786432
  64.0 0.7 %copy.18 = bf16[6,3,4096]{2,1,0:T(4,128)(2,1)} copy(bf16[6,3,4096]{2,1,0:T(4,128)(2,1)S(1)} %get-tuple-element.5) | data formatting | bytes 294912
  64.6 0.9 %copy.17 = bf16[12,6,4096]{2,1,0:T(8,128)(2,1)} copy(bf16[12,6,4096]{2,1,0:T(8,128)(2,1)S(1)} %get-tuple-element.4) | data formatting | bytes 1179648

commit v4 on v3

--- a/solution.py
+++ b/solution.py
@@ -147,6 +147,8 @@
     rank = change.shape[1]
     part = count // 2
     chunk = parent_count // 2
+    pieces = 3
+    share = parent_count // pieces
     sub, grp = lax.axis_index("sub"), lax.axis_index("grp")
     across, along, core = sub // (2 * SIDE), (sub // 2) % SIDE, sub % 2
     member = core
@@ -227,13 +229,13 @@
         return send_leaf(number, leaves.at[pl.ds(start, size)], start, size, target)
 
     def send_parent(way, step, piece):
-        number = (way * (groups // 2) + step) * 2 + piece
+        number = (way * (groups // 2) + step) * pieces + piece
         origin = (grp - step + groups) % groups if way == 0 else (grp + step) % groups
-        at = origin * parent_count + piece * chunk
-        src = parent_change.at[pl.ds(piece * chunk, chunk)] if step == 0 else parents.at[pl.ds(at, chunk)]
+        at = origin * parent_count + piece * share
+        src = parent_change.at[pl.ds(piece * share, share)] if step == 0 else parents.at[pl.ds(at, share)]
         copy = pltpu.make_async_remote_copy(
             src_ref=src,
-            dst_ref=parents.at[pl.ds(at, chunk)],
+            dst_ref=parents.at[pl.ds(at, share)],
             send_sem=ring_send.at[number],
             recv_sem=ring_recv.at[number],
             device_id={"grp": up if way == 0 else down},
@@ -245,7 +247,7 @@
 
     loads[0].wait()
 
-    @pl.loop(0, parent_count, unroll=3)
+    @pl.loop(0, parent_count, unroll=6)
     def _(p):
         total = nt(parent_blocks_ref[p, 0], parent_blocks_ref[p, 0])
         for c in range(1, parent_links):
@@ -271,20 +273,20 @@
         weight = weight + nt(beside(*split(carried)), twice)
         image_high[which * part + p], image_low[which * part + p] = image_of(start, weight)
 
-    @pl.loop(0, part, unroll=3)
+    @pl.loop(0, part, unroll=6)
     def _(p):
         leaf_image(0, p, weight_high[p], weight_low[p])
 
     other_sent.wait_recv()
 
-    @pl.loop(0, part, unroll=3)
+    @pl.loop(0, part, unroll=6)
     def _(p):
         leaf_image(1, p, other_weight[p], None)
 
     def leaf_terms(which, p):
         return image_high[which * part + p], image_low[which * part + p]
 
-    @pl.loop(0, part, unroll=3)
+    @pl.loop(0, part, unroll=6)
     def _(p):
         grams[p] = gram_pair(leaf_terms(0, p), leaf_terms(1, p))
 
@@ -292,7 +294,7 @@
 
     own_start = [block_start(h, outer_at[h], inner_at[h]) for h in range(2)]
 
-    @pl.loop(0, part, unroll=3)
+    @pl.loop(0, part, unroll=6)
     def _(p):
         both = rows_pair(grams[p], leaf_terms(0, p), leaf_terms(1, p))
         for which in range(2):
@@ -316,7 +318,7 @@
 
     loads[3].wait()
 
-    @pl.loop(0, count, unroll=3)
+    @pl.loop(0, count, unroll=6)
     def _(t):
         bases_out[t] = nt(change[t], bases_ref[t]).astype(BF16)
 
@@ -324,7 +326,7 @@
     parent_start = split(parent_start_ref[...])
     first = member == 0
 
-    @pl.loop(0, parent_count, unroll=3)
+    @pl.loop(0, parent_count, unroll=6)
     def _(p):
         mine, other = kept[p], received[p].astype(F32)
         stacked = split(above(jnp.where(first, mine, other), jnp.where(first, other, mine)))
@@ -366,17 +368,17 @@
             parents[grp * parent_count + q] = rows
 
     ring = {}
-    for piece in range(2):
+    for piece in range(pieces):
         for way in range(2):
             ring[way, 0, piece] = send_parent(way, 0, piece)
 
     def ring_step(step):
-        for piece in range(2):
+        for piece in range(pieces):
             for way in range(2):
                 if (way, step, piece) not in ring:
                     continue
                 ring[way, step, piece].wait_recv()
-                if step < groups // 2 - 2 or (step == groups // 2 - 2 and way == piece):
+                if step < groups // 2 - 2 or (step == groups // 2 - 2 and way == 2 * piece // pieces):
                     ring[way, step + 1, piece] = send_parent(way, step + 1, piece)
 
     for h in range(2):
@@ -401,7 +403,7 @@
     order = jnp.where(row < low, 2 * row, 2 * (row - low) + 1)
     shuffle = jnp.where(column == order, 1.0, 0.0).astype(BF16)
 
-    @pl.loop(0, parent_count, unroll=3)
+    @pl.loop(0, parent_count, unroll=6)
     def _(p):
         mixed = nn(shuffle, parent_change[p]).astype(BF16)
         for c in range(parent_links):
@@ -517,7 +519,7 @@
     whole, outside = pl.BlockSpec(memory_space=pltpu.VMEM), pl.BlockSpec(memory_space=pl.ANY)
     indices = (leaf_partner_dev.T, leaf_partner_slot.T, parent_partner_group.T, parent_partner_slot.T)
     streams = (leaf_bases, leaf_transfers, leaf_blocks, parent_blocks)
-    transfers = (2, 28, 4 * groups // 2)
+    transfers = (2, 28, 3 * groups)
     return pl.pallas_call(
         functools.partial(kernel, groups),
         out_shape=(

time: 65.7 us -> 65.2 us (level)
  no operation moved by 1% of the time
where the time goes in v4:
time: 65.2 us; the launch traced here: 65 us
  Pallas kernels  62.1 us (95%)
  local copies, waits for them, and re-layouts  2.3 us (4%)
    pallas_call x1, Pallas kernels, shards(): pl.pallas_call(functools.partial(kernel, groups), out_shape=(shape(leaf_c...  62.1 us
    unnamed x3, local copies, waits for them, and re-layouts  2.3 us

profile of v4, /device:TPU:1, one launch (start us, length us, event | category | flops | bytes accessed | tf_op | source)
XLA Modules:
  0.0 65.0 jit_solution(4432513239178495900)
XLA Ops:
  0.6 62.1 %recompress.1 = (bf16[12,64,256]{2,1,0:T(8,128)(2,1)S(1)}, bf16[12,6,4096]{2,1,0:T(8,128)(2,1)S(1)}, bf16[6,3,4096]{2,1,0:T(4,128)(2,1)S(1)}) custom-call(s32[6,12]{1,0:T(8,128)} %bitcast.4, s32[6,12]{1,0:T(8,128)} %bitcast.5, s32[3,6]{1,0:T(4,128)} %bitcast.6, s32[3,6]{1,0:T(4,128)} %bitcast.7, f32[64,128]{1,0:T(8,128)} %leaf_start_ref.1, ...), custom_call_target="tpu_custom_call" | custom-call | tf_op jit(solution)/shard_map/recompress/pallas_call | solution.py:523
  62.7 0.7 %copy.16 = bf16[12,64,256]{2,1,0:T(8,128)(2,1)} copy(bf16[12,64,256]{2,1,0:T(8,128)(2,1)S(1)} %get-tuple-element.3) | data formatting | bytes 786432
  63.5 0.7 %copy.18 = bf16[6,3,4096]{2,1,0:T(4,128)(2,1)} copy(bf16[6,3,4096]{2,1,0:T(4,128)(2,1)S(1)} %get-tuple-element.5) | data formatting | bytes 294912
  64.2 0.9 %copy.17 = bf16[12,6,4096]{2,1,0:T(8,128)(2,1)} copy(bf16[12,6,4096]{2,1,0:T(8,128)(2,1)S(1)} %get-tuple-element.4) | data formatting | bytes 1179648
